TPU v7x, 32 devices: a whole 2x2x4 slice. The times are simulated.
32 devices in a mesh: section: 4 (over y, x), row: 8 (over z, core).
Axes of the slice: x: 2, y: 2, z: 4, core: 2. Of those that a mesh axis runs over, the one named last changes fastest.
Arguments:
- in_flight: bfloat16 [2, 4, 16, 128, 256], P(None, 'section', 'row'), may hold values from -6 to 6
- fresh: bfloat16 [2, 3, 16, 128, 256], P(None, None, 'row'), may hold values from -6 to 6
- saved_inputs: bfloat16 [2, 4, 4, 16, 128, 256], P(None, None, 'section', 'row'), may hold values from -6 to 6
- saved_hidden: bfloat16 [2, 4, 4, 16, 128, 256], P(None, None, 'section', 'row'), may hold values from 0 to 2
- masks: int32 [2, 4, 4, 2, 16, 16, 256], P(None, None, 'section', None, 'row'), may hold values from 0 to 255
- weights: bfloat16 [4, 2, 2304, 256], P('section'), may hold values from -0.125 to 0.125
Outputs:
- grads: bfloat16 [2, 4, 4, 16, 128, 256], P(None, None, 'section', 'row')
- weight_grads: float32 [4, 2, 2304, 256], P('section', None, 'row')
Inputs may be any that keep to these rules, and one draw needn't show every extreme that they name: `masks`: bit q of entry [r, t, p, k, i, j, c] is the gate at image row i, column 8 j + q, channel c; k = 0 gates the first convolution's output, k = 1 the residual sum.
All inputs are finite; a program needn't handle non-finite values.
Results may differ from a plain program's by a relative error of at most 0.014.
Values may be sent and summed in bfloat16 or wider, within the bound.
A program may use at most 192 MiB of HBM per device.

v0:
```python
import functools
import math

import jax
import jax.numpy as jnp
from jax import lax
from jax.experimental import pallas as pl
from jax.experimental.pallas import tpu as pltpu
from jax.sharding import PartitionSpec as P

F32 = jnp.float32
BF16 = jnp.bfloat16
VMEM = pl.BlockSpec(memory_space=pltpu.VMEM)
SMEM = pl.BlockSpec(memory_space=pltpu.SMEM)


def gate_of(words):
    groups, channels = words.shape
    bit = lax.broadcasted_iota(jnp.int32, (8, channels), 0)
    pieces = [
        jnp.bitwise_and(
            jnp.right_shift(jnp.broadcast_to(words[j : j + 1, :], (8, channels)), bit), 1
        )
        for j in range(groups)
    ]
    return jnp.concatenate(pieces, axis=0).astype(F32)


def shifted(x, step):
    cols = x.shape[0]
    rolled = pltpu.roll(x, (-step) % cols, 0)
    at = lax.broadcasted_iota(jnp.int32, x.shape, 0)
    edge = cols - 1 if step == 1 else 0
    return jnp.where(at == edge, 0.0, rolled)


def gate_kernel(last_ref, handed_ref, fresh_ref, words_ref, out_ref):
    replicas, rows = out_ref.shape[:2]
    is_last = last_ref[0] == 1
    for r in range(replicas):
        for i in range(rows):
            state = jnp.where(is_last, fresh_ref[r, i].astype(F32), handed_ref[r, i].astype(F32))
            out_ref[r, i] = (state * gate_of(words_ref[r, i])).astype(BF16)


def transposed(core_ref, above_ref, below_ref, w_ref):
    replicas, rows, cols, channels = core_ref.shape
    padded = [
        [above_ref[r]] + [core_ref[r, i] for i in range(rows)] + [below_ref[r]]
        for r in range(replicas)
    ]
    lhs = jnp.concatenate(
        [
            jnp.concatenate(
                [padded[r][i - u + 2] for r in range(replicas) for i in range(rows)], axis=0
            )
            for u in range(3)
        ],
        axis=1,
    )
    parts = []
    for v in range(3):
        rhs = jnp.concatenate(
            [w_ref[pl.ds((u * 3 + v) * channels, channels), :] for u in range(3)], axis=1
        )
        parts.append(
            lax.dot_general(lhs, rhs, (((1,), (1,)), ((), ())), preferred_element_type=F32)
        )
    out = []
    for n in range(replicas * rows):
        low, mid, high = (part[n * cols : (n + 1) * cols] for part in parts)
        out.append(shifted(low, 1) + mid + shifted(high, -1))
    return out


def mid_kernel(core_ref, above_ref, below_ref, w_ref, words_ref, out_ref):
    replicas, rows = core_ref.shape[:2]
    back = transposed(core_ref, above_ref, below_ref, w_ref)
    for r in range(replicas):
        for i in range(rows):
            out_ref[r, i] = (back[r * rows + i] * gate_of(words_ref[r, i])).astype(BF16)


def out_kernel(core_ref, above_ref, below_ref, w_ref, skip_ref, out_ref):
    replicas, rows = core_ref.shape[:2]
    back = transposed(core_ref, above_ref, below_ref, w_ref)
    for r in range(replicas):
        for i in range(rows):
            out_ref[r, i] = (skip_ref[r, i].astype(F32) + back[r * rows + i]).astype(BF16)


def grad_kernel(ticks, *refs):
    own_ref, other_ref = refs[:2]
    cores = refs[2 : 2 + ticks]
    aboves = refs[2 + ticks : 2 + 2 * ticks]
    belows = refs[2 + 2 * ticks : 2 + 3 * ticks]
    out_ref = refs[2 + 3 * ticks]
    xt_ref = refs[3 + 3 * ticks]
    y_ref = refs[4 + 3 * ticks]
    replicas, rows, cols, channels = cores[0].shape
    span = replicas * rows * cols
    for t in range(ticks):
        for r in range(replicas):
            for i in range(rows):
                x = (own_ref if r == 0 else other_ref)[t, i]
                at = t * span + (r * rows + i) * cols
                xt_ref[:, at : at + cols] = x.T
    for v in range(3):
        for t in range(ticks):
            for r in range(replicas):
                padded = [aboves[t][r]] + [cores[t][r, i] for i in range(rows)] + [belows[t][r]]
                for n in range(rows + 2):
                    line = padded[n]
                    if v != 1:
                        line = shifted(line.astype(F32), 1 - v).astype(BF16)
                    for u in range(3):
                        i = n + u - 2
                        if 0 <= i < rows:
                            at = t * span + (r * rows + i) * cols
                            y_ref[at : at + cols, u * channels : (u + 1) * channels] = line
        term = jnp.dot(xt_ref[...], y_ref[...], preferred_element_type=F32)
        for u in range(3):
            out_ref[(u * 3 + v) * channels : (u * 3 + v + 1) * channels, :] = term[
                :, u * channels : (u + 1) * channels
            ].astype(BF16)


def params(limit):
    return pltpu.CompilerParams(vmem_limit_bytes=limit << 20)


def call(kernel, out_shape, flops, *operands, specs=None, scratch=(), limit=24):
    moved = sum(math.prod(o.shape) * o.dtype.itemsize for o in operands)
    return pl.pallas_call(
        kernel,
        out_shape=out_shape,
        in_specs=specs or [VMEM] * len(operands),
        out_specs=VMEM,
        scratch_shapes=scratch,
        compiler_params=params(limit),
        cost_estimate=pl.CostEstimate(flops=flops, bytes_accessed=moved, transcendentals=0),
    )(*operands)


def edges(x):
    size = lax.axis_size("row")
    down = [(i, i + 1) for i in range(size - 1)]
    up = [(j, i) for i, j in down]
    return lax.ppermute(x[:, -1], "row", down), lax.ppermute(x[:, 0], "row", up)


def mirrored(x):
    size = lax.axis_size("section")
    return lax.ppermute(x, "section", [(i, size - 1 - i) for i in range(size)])


def per_device(in_flight, fresh, saved_inputs, saved_hidden, masks, weights):
    sections = lax.axis_size("section")
    bands = lax.axis_size("row")
    position = lax.axis_index("section")
    replicas, ticks = saved_inputs.shape[:2]
    rows, cols, channels = saved_inputs.shape[3:]
    w1, w2 = weights[0, 0], weights[0, 1]
    own_masks = masks[0, :, 0]
    other_flight = mirrored(in_flight[1, 0])
    other_masks = [mirrored(masks[1, t, 0]) for t in range(ticks)]
    other_hidden = mirrored(saved_hidden[1, :, 0])
    other_inputs = mirrored(saved_inputs[1, :, 0])
    is_last = (position == sections - 1).astype(jnp.int32).reshape(1)
    below = [(i, i - 1) for i in range(1, sections)]
    shape = jax.ShapeDtypeStruct((replicas, rows, cols, channels), BF16)
    conv_flops = 2 * replicas * rows * cols * 9 * channels * channels
    handed = jnp.stack([in_flight[0, 0], other_flight])
    lines = []
    outs = [[], []]
    for t in range(ticks):
        words = jnp.stack([own_masks[t], other_masks[t]])
        entering = handed if t == 0 else fresh[:, t - 1]
        g2 = call(
            gate_kernel, shape, 1, is_last, handed, entering, words[:, 1],
            specs=[SMEM, VMEM, VMEM, VMEM],
        )
        a2, b2 = edges(g2)
        g1 = call(mid_kernel, shape, conv_flops, g2, a2, b2, w2, words[:, 0])
        a1, b1 = edges(g1)
        produced = call(out_kernel, shape, conv_flops, g1, a1, b1, w1, g2)
        if t < ticks - 1:
            handed = lax.ppermute(produced, "section", below)
        outs[0].append(produced[0])
        outs[1].append(mirrored(produced[1]))
        lines.append((g2, a2, b2, g1, a1, b1))
    scale = 1.0 / math.sqrt(replicas * ticks * rows * bands * cols)
    span = replicas * rows * cols * ticks
    scratch = [pltpu.VMEM((channels, span), BF16), pltpu.VMEM((span, 3 * channels), BF16)]
    term_shape = jax.ShapeDtypeStruct((9 * channels, channels), BF16)

    def term(own, other, first):
        return call(
            functools.partial(grad_kernel, ticks), term_shape, conv_flops * ticks,
            own, other,
            *[l[first] for l in lines], *[l[first + 1] for l in lines], *[l[first + 2] for l in lines],
            scratch=scratch, limit=40,
        )

    def scattered(x):
        return lax.psum_scatter(x, "row", scatter_dimension=0, tiled=True).astype(F32) * scale

    second = scattered(term(saved_hidden[0, :, 0], other_hidden, 0))
    first = scattered(term(saved_inputs[0, :, 0], other_inputs, 3))
    grads = jnp.stack([jnp.stack(o) for o in outs])[:, :, None]
    return grads, jnp.stack([first, second])[None]


def solution(mesh):
    return jax.shard_map(
        per_device,
        mesh=mesh,
        in_specs=(
            P(None, "section", "row", None, None),
            P(None, None, "row", None, None),
            P(None, None, "section", "row", None, None),
            P(None, None, "section", "row", None, None),
            P(None, None, "section", None, "row", None, None),
            P("section", None, None, None),
        ),
        out_specs=(P(None, None, "section", "row", None, None), P("section", None, "row", None)),
        check_vma=False,
    )
```

profile of v0, /device:TPU:0, one launch (start us, length us, event | category | flops | bytes accessed | tf_op | source)
XLA Modules:
  0.0 200.8 jit_solution(14405310845827453173)
XLA Ops:
  9.0 3.9 %collective-permute-start.1 = (s32[2,2,16,256]{3,2,1,0:T(8,128)S(1)}, s32[2,2,16,256]{3,2,1,0:T(8,128)S(1)}, u32[]{:S(2)}, u32[]{:S(2)}) collective-permute-start(s32[2,2,16,256]{3,2,1,0:T(8,128)S(1)} %get-tuple-element.18), channel_id=1, source_target_pairs={{0,24},{8,16},{16,8},{24,0},{1,25},{9,17},{17,9},{25,1},{2,26},{10... | collective-permute-start | bytes 196616 | tf_op jit(solution)/shard_map/ppermute | solution.py:154
  15.4 3.5 %collective-permute-done = bf16[2,128,256]{2,1,0:T(8,128)(2,1)S(1)} collective-permute-done((bf16[2,128,256]{2,1,0:T(8,128)(2,1)S(1)}, bf16[2,128,256]{2,1,0:T(8,128)(2,1)S(1)}, u32[]{:S(2)}, u32[]{:S(2)}) %collective-permute-start) | collective-permute-done | bytes 131104 | tf_op jit(solution)/shard_map/ppermute | solution.py:154
  26.3 5.6 %collective-permute-start.4 = (bf16[2,128,256]{2,1,0:T(8,128)(2,1)S(1)}, bf16[2,128,256]{2,1,0:T(8,128)(2,1)S(1)}, u32[]{:S(2)}, u32[]{:S(2)}) collective-permute-start(bf16[2,128,256]{2,1,0:T(8,128)(2,1)S(1)} %get-tuple-element.42), channel_id=1, source_target_pairs={{0,1},{1,2},{2,3},{3,4},{4,5},{5,6},{6,7},{8,9},{9,10},{10,11},{11... | collective-permute-start | bytes 393224 | tf_op jit(solution)/shard_map/ppermute | solution.py:149
  39.2 5.5 %collective-permute-done.6.handed_ref = bf16[2,2,128,256]{3,2,1,0:T(8,128)(2,1)S(1)} collective-permute-done((bf16[2,2,128,256]{3,2,1,0:T(8,128)(2,1)S(1)}, bf16[2,2,128,256]{3,2,1,0:T(8,128)(2,1)S(1)}, u32[]{:S(2)}, u32[]{:S(2)}) %collective-permute-start.6) | collective-permute-done | bytes 262176 | tf_op jit(solution)/shard_map/ppermute | solution.py:188
  44.8 4.1 %collective-permute-start.8 = (bf16[2,128,256]{2,1,0:T(8,128)(2,1)S(1)}, bf16[2,128,256]{2,1,0:T(8,128)(2,1)S(1)}, u32[]{:S(2)}, u32[]{:S(2)}) collective-permute-start(bf16[2,128,256]{2,1,0:T(8,128)(2,1)S(1)} %get-tuple-element.40), channel_id=1, source_target_pairs={{0,1},{1,2},{2,3},{3,4},{4,5},{5,6},{6,7},{8,9},{9,10},{10,11},{11... | collective-permute-start | bytes 393224 | tf_op jit(solution)/shard_map/ppermute | solution.py:149
  50.3 3.7 %collective-permute-done.9.below_ref.refs_11_ = bf16[2,128,256]{2,1,0:T(8,128)(2,1)S(1)} collective-permute-done((bf16[2,128,256]{2,1,0:T(8,128)(2,1)S(1)}, bf16[2,128,256]{2,1,0:T(8,128)(2,1)S(1)}, u32[]{:S(2)}, u32[]{:S(2)}) %collective-permute-start.9) | collective-permute-done | bytes 131104 | tf_op jit(solution)/shard_map/ppermute | solution.py:149
  54.8 5.6 %collective-permute-start.10 = (bf16[2,128,256]{2,1,0:T(8,128)(2,1)S(1)}, bf16[2,128,256]{2,1,0:T(8,128)(2,1)S(1)}, u32[]{:S(2)}, u32[]{:S(2)}) collective-permute-start(bf16[2,128,256]{2,1,0:T(8,128)(2,1)S(1)} %get-tuple-element.38), channel_id=1, source_target_pairs={{0,1},{1,2},{2,3},{3,4},{4,5},{5,6},{6,7},{8,9},{9,10},{10,11},{11... | collective-permute-start | bytes 393224 | tf_op jit(solution)/shard_map/ppermute | solution.py:149
  65.8 3.3 %collective-permute-start.13 = (s32[2,2,16,256]{3,2,1,0:T(8,128)S(1)}, s32[2,2,16,256]{3,2,1,0:T(8,128)S(1)}, u32[]{:S(2)}, u32[]{:S(2)}) collective-permute-start(s32[2,2,16,256]{3,2,1,0:T(8,128)S(1)} %copy-done.28), channel_id=1, source_target_pairs={{0,24},{8,16},{16,8},{24,0},{1,25},{9,17},{17,9},{25,1},{2,26},{10... | collective-permute-start | bytes 196616 | tf_op jit(solution)/shard_map/ppermute | solution.py:154
  69.0 6.4 %collective-permute-done.13 = s32[2,2,16,256]{3,2,1,0:T(8,128)S(1)} collective-permute-done((s32[2,2,16,256]{3,2,1,0:T(8,128)S(1)}, s32[2,2,16,256]{3,2,1,0:T(8,128)S(1)}, u32[]{:S(2)}, u32[]{:S(2)}) %collective-permute-start.13) | collective-permute-done | bytes 65568 | tf_op jit(solution)/shard_map/ppermute | solution.py:154
  75.6 3.8 %collective-permute-start.14 = (bf16[2,128,256]{2,1,0:T(8,128)(2,1)S(1)}, bf16[2,128,256]{2,1,0:T(8,128)(2,1)S(1)}, u32[]{:S(2)}, u32[]{:S(2)}) collective-permute-start(bf16[2,128,256]{2,1,0:T(8,128)(2,1)S(1)} %get-tuple-element.36), channel_id=1, source_target_pairs={{0,1},{1,2},{2,3},{3,4},{4,5},{5,6},{6,7},{8,9},{9,10},{10,11},{11... | collective-permute-start | bytes 393224 | tf_op jit(solution)/shard_map/ppermute | solution.py:149
  80.8 3.7 %collective-permute-done.15.below_ref.refs_12_ = bf16[2,128,256]{2,1,0:T(8,128)(2,1)S(1)} collective-permute-done((bf16[2,128,256]{2,1,0:T(8,128)(2,1)S(1)}, bf16[2,128,256]{2,1,0:T(8,128)(2,1)S(1)}, u32[]{:S(2)}, u32[]{:S(2)}) %collective-permute-start.15) | collective-permute-done | bytes 131104 | tf_op jit(solution)/shard_map/ppermute | solution.py:149
  85.3 5.6 %collective-permute-start.16 = (bf16[2,128,256]{2,1,0:T(8,128)(2,1)S(1)}, bf16[2,128,256]{2,1,0:T(8,128)(2,1)S(1)}, u32[]{:S(2)}, u32[]{:S(2)}) collective-permute-start(bf16[2,128,256]{2,1,0:T(8,128)(2,1)S(1)} %get-tuple-element.34), channel_id=1, source_target_pairs={{0,1},{1,2},{2,3},{3,4},{4,5},{5,6},{6,7},{8,9},{9,10},{10,11},{11... | collective-permute-start | bytes 393224 | tf_op jit(solution)/shard_map/ppermute | solution.py:149
  96.4 4.1 %collective-permute-start.29 = (bf16[4,2,128,256]{3,2,1,0:T(8,128)(2,1)S(1)}, bf16[4,2,128,256]{3,2,1,0:T(8,128)(2,1)S(1)}, u32[]{:S(2)}, u32[]{:S(2)}) collective-permute-start(bf16[4,2,128,256]{3,2,1,0:T(8,128)(2,1)S(1)} %get-tuple-element.8), channel_id=1, source_target_pairs={{0,24},{8,16},{16,8},{24,0},{1,25},{9,17},{17,9},{25,1},{2,26},{10... | collective-permute-start | bytes 1572872 | tf_op jit(solution)/shard_map/ppermute | solution.py:154
  100.5 3.0 %collective-permute-done.18.handed_ref = bf16[2,2,128,256]{3,2,1,0:T(8,128)(2,1)S(1)} collective-permute-done((bf16[2,2,128,256]{3,2,1,0:T(8,128)(2,1)S(1)}, bf16[2,2,128,256]{3,2,1,0:T(8,128)(2,1)S(1)}, u32[]{:S(2)}, u32[]{:S(2)}) %collective-permute-start.18) | collective-permute-done | bytes 262176 | tf_op jit(solution)/shard_map/ppermute | solution.py:188
  103.7 8.1 %collective-permute-start.20 = (bf16[2,128,256]{2,1,0:T(8,128)(2,1)S(1)}, bf16[2,128,256]{2,1,0:T(8,128)(2,1)S(1)}, u32[]{:S(2)}, u32[]{:S(2)}) collective-permute-start(bf16[2,128,256]{2,1,0:T(8,128)(2,1)S(1)} %get-tuple-element.32), channel_id=1, source_target_pairs={{0,1},{1,2},{2,3},{3,4},{4,5},{5,6},{6,7},{8,9},{9,10},{10,11},{11... | collective-permute-start | bytes 393224 | tf_op jit(solution)/shard_map/ppermute | solution.py:149
  113.1 3.7 %collective-permute-done.29.refs_1_ = bf16[4,2,128,256]{3,2,1,0:T(8,128)(2,1)S(1)} collective-permute-done((bf16[4,2,128,256]{3,2,1,0:T(8,128)(2,1)S(1)}, bf16[4,2,128,256]{3,2,1,0:T(8,128)(2,1)S(1)}, u32[]{:S(2)}, u32[]{:S(2)}) %collective-permute-start.29) | collective-permute-done | bytes 524320 | tf_op jit(solution)/shard_map/ppermute | solution.py:154
  116.9 3.8 %shard_map.90 = bf16[2304,256]{1,0:T(8,128)(2,1)} custom-call(bf16[4,2,128,256]{3,2,1,0:T(8,128)(2,1)S(1)} %get-tuple-element.9.refs_0_, bf16[4,2,128,256]{3,2,1,0:T(8,128)(2,1)S(1)} %collective-permute-done.29.refs_1_, bf16[2,2,128,256]{3,2,1,0:T(8,128)(2,1)S(1)} %shard_map.77.core_ref.skip_ref.refs_2_, ...), custom_call_target="tpu_custom_call" | custom-call | flops 2415919104 | bytes 3145728 | tf_op jit(solution)/shard_map/pallas_call | solution.py:134
  124.5 3.5 %collective-permute-start.22 = (bf16[2,128,256]{2,1,0:T(8,128)(2,1)S(1)}, bf16[2,128,256]{2,1,0:T(8,128)(2,1)S(1)}, u32[]{:S(2)}, u32[]{:S(2)}) collective-permute-start(bf16[2,128,256]{2,1,0:T(8,128)(2,1)S(1)} %get-tuple-element.30), channel_id=1, source_target_pairs={{0,1},{1,2},{2,3},{3,4},{4,5},{5,6},{6,7},{8,9},{9,10},{10,11},{11... | collective-permute-start | bytes 393224 | tf_op jit(solution)/shard_map/ppermute | solution.py:149
  129.5 9.0 %collective-permute-done.28.refs_1_ = bf16[4,2,128,256]{3,2,1,0:T(8,128)(2,1)S(1)} collective-permute-done((bf16[4,2,128,256]{3,2,1,0:T(8,128)(2,1)S(1)}, bf16[4,2,128,256]{3,2,1,0:T(8,128)(2,1)S(1)}, u32[]{:S(2)}, u32[]{:S(2)}) %collective-permute-start.28) | collective-permute-done | bytes 524320 | tf_op jit(solution)/shard_map/ppermute | solution.py:154
  138.6 3.8 %shard_map.89 = bf16[2304,256]{1,0:T(8,128)(2,1)} custom-call(bf16[4,2,128,256]{3,2,1,0:T(8,128)(2,1)S(1)} %get-tuple-element.7.refs_0_, bf16[4,2,128,256]{3,2,1,0:T(8,128)(2,1)S(1)} %collective-permute-done.28.refs_1_, bf16[2,2,128,256]{3,2,1,0:T(8,128)(2,1)S(1)} %shard_map.78.core_ref.refs_2_, bf16[2,2,128,256]{3,2,1,0:T(8,128)(2,1)S(1)} %copy-done.1, ...), custom_call_target="tpu_custom_call" | custom-call | flops 2415919104 | bytes 3145728 | tf_op jit(solution)/shard_map/pallas_call | solution.py:134
  142.6 3.0 %collective-permute-start.25 = (bf16[2,128,256]{2,1,0:T(8,128)(2,1)S(1)}, bf16[2,128,256]{2,1,0:T(8,128)(2,1)S(1)}, u32[]{:S(2)}, u32[]{:S(2)}) collective-permute-start(bf16[2,128,256]{2,1,0:T(8,128)(2,1)S(1)} %get-tuple-element.24), channel_id=1, source_target_pairs={{0,24},{8,16},{16,8},{24,0},{1,25},{9,17},{17,9},{25,1},{2,26},{10... | collective-permute-start | bytes 393224 | tf_op jit(solution)/shard_map/ppermute | solution.py:154
  146.5 3.0 %collective-permute-start.27 = (bf16[2,128,256]{2,1,0:T(8,128)(2,1)S(1)}, bf16[2,128,256]{2,1,0:T(8,128)(2,1)S(1)}, u32[]{:S(2)}, u32[]{:S(2)}) collective-permute-start(bf16[2,128,256]{2,1,0:T(8,128)(2,1)S(1)} %get-tuple-element.28), channel_id=1, source_target_pairs={{0,24},{8,16},{16,8},{24,0},{1,25},{9,17},{17,9},{25,1},{2,26},{10... | collective-permute-start | bytes 393224 | tf_op jit(solution)/shard_map/ppermute | solution.py:154
  152.6 2.8 %collective-permute-done.26 = bf16[2,128,256]{2,1,0:T(8,128)(2,1)S(1)} collective-permute-done((bf16[2,128,256]{2,1,0:T(8,128)(2,1)S(1)}, bf16[2,128,256]{2,1,0:T(8,128)(2,1)S(1)}, u32[]{:S(2)}, u32[]{:S(2)}) %collective-permute-start.26) | collective-permute-done | bytes 131104 | tf_op jit(solution)/shard_map/ppermute | solution.py:154
  159.9 32.3 %reduce-scatter.3.cloned.1.call-done = bf16[288,256]{1,0:T(8,128)(2,1)} async-done(((bf16[2304,256]{1,0:T(8,128)(2,1)}), bf16[288,256]{1,0:T(8,128)(2,1)}) %reduce-scatter.3.cloned.1.call-update) | async-done | bytes 147472 | tf_op jit(solution)/shard_map/reduce_scatter | solution.py:206
  (143 shorter events, 51.3 us)
Async XLA Ops:
  7.2 151.8 %reduce-scatter.5.cloned.1.call-start = ((), (), s32[]{:S(2)}) async-start(), calls=%async_computation.3 | async-start | bytes 1327104 | tf_op jit(solution)/shard_map/reduce_scatter | solution.py:206
  9.0 6.4 %collective-permute-start.1 = (s32[2,2,16,256]{3,2,1,0:T(8,128)S(1)}, s32[2,2,16,256]{3,2,1,0:T(8,128)S(1)}, u32[]{:S(2)}, u32[]{:S(2)}) collective-permute-start(s32[2,2,16,256]{3,2,1,0:T(8,128)S(1)} %get-tuple-element.18), channel_id=1, source_target_pairs={{0,24},{8,16},{16,8},{24,0},{1,25},{9,17},{17,9},{25,1},{2,26},{10... | collective-permute-start | bytes 196616 | tf_op jit(solution)/shard_map/ppermute | solution.py:154
  13.0 5.9 %collective-permute-start = (bf16[2,128,256]{2,1,0:T(8,128)(2,1)S(1)}, bf16[2,128,256]{2,1,0:T(8,128)(2,1)S(1)}, u32[]{:S(2)}, u32[]{:S(2)}) collective-permute-start(bf16[2,128,256]{2,1,0:T(8,128)(2,1)S(1)} %get-tuple-element.46), channel_id=1, source_target_pairs={{0,24},{8,16},{16,8},{24,0},{1,25},{9,17},{17,9},{25,1},{2,26},{10... | collective-permute-start | bytes 393224 | tf_op jit(solution)/shard_map/ppermute | solution.py:154
  26.3 8.5 %collective-permute-start.4 = (bf16[2,128,256]{2,1,0:T(8,128)(2,1)S(1)}, bf16[2,128,256]{2,1,0:T(8,128)(2,1)S(1)}, u32[]{:S(2)}, u32[]{:S(2)}) collective-permute-start(bf16[2,128,256]{2,1,0:T(8,128)(2,1)S(1)} %get-tuple-element.42), channel_id=1, source_target_pairs={{0,1},{1,2},{2,3},{3,4},{4,5},{5,6},{6,7},{8,9},{9,10},{10,11},{11... | collective-permute-start | bytes 393224 | tf_op jit(solution)/shard_map/ppermute | solution.py:149
  33.2 6.0 %collective-permute-start.7 = (s32[2,2,16,256]{3,2,1,0:T(8,128)}, s32[2,2,16,256]{3,2,1,0:T(8,128)S(1)}, u32[]{:S(2)}, u32[]{:S(2)}) collective-permute-start(s32[2,2,16,256]{3,2,1,0:T(8,128)} %get-tuple-element.16), channel_id=1, source_target_pairs={{0,24},{8,16},{16,8},{24,0},{1,25},{9,17},{17,9},{25,1},{2,26},{10... | collective-permute-start | bytes 196616 | tf_op jit(solution)/shard_map/ppermute | solution.py:154
  36.0 8.7 %collective-permute-start.6 = (bf16[2,2,128,256]{3,2,1,0:T(8,128)(2,1)S(1)}, bf16[2,2,128,256]{3,2,1,0:T(8,128)(2,1)S(1)}, u32[]{:S(2)}, u32[]{:S(2)}) collective-permute-start(bf16[2,2,128,256]{3,2,1,0:T(8,128)(2,1)S(1)} %shard_map.79), channel_id=1, source_target_pairs={{8,0},{16,8},{24,16},{9,1},{17,9},{25,17},{10,2},{18,10},{26,18},{... | collective-permute-start | bytes 786440 | tf_op jit(solution)/shard_map/ppermute | solution.py:188
  44.8 5.4 %collective-permute-start.8 = (bf16[2,128,256]{2,1,0:T(8,128)(2,1)S(1)}, bf16[2,128,256]{2,1,0:T(8,128)(2,1)S(1)}, u32[]{:S(2)}, u32[]{:S(2)}) collective-permute-start(bf16[2,128,256]{2,1,0:T(8,128)(2,1)S(1)} %get-tuple-element.40), channel_id=1, source_target_pairs={{0,1},{1,2},{2,3},{3,4},{4,5},{5,6},{6,7},{8,9},{9,10},{10,11},{11... | collective-permute-start | bytes 393224 | tf_op jit(solution)/shard_map/ppermute | solution.py:149
  54.8 6.9 %collective-permute-start.10 = (bf16[2,128,256]{2,1,0:T(8,128)(2,1)S(1)}, bf16[2,128,256]{2,1,0:T(8,128)(2,1)S(1)}, u32[]{:S(2)}, u32[]{:S(2)}) collective-permute-start(bf16[2,128,256]{2,1,0:T(8,128)(2,1)S(1)} %get-tuple-element.38), channel_id=1, source_target_pairs={{0,1},{1,2},{2,3},{3,4},{4,5},{5,6},{6,7},{8,9},{9,10},{10,11},{11... | collective-permute-start | bytes 393224 | tf_op jit(solution)/shard_map/ppermute | solution.py:149
  64.5 11.0 %collective-permute-start.12 = (bf16[2,2,128,256]{3,2,1,0:T(8,128)(2,1)S(1)}, bf16[2,2,128,256]{3,2,1,0:T(8,128)(2,1)S(1)}, u32[]{:S(2)}, u32[]{:S(2)}) collective-permute-start(bf16[2,2,128,256]{3,2,1,0:T(8,128)(2,1)S(1)} %shard_map.82), channel_id=1, source_target_pairs={{8,0},{16,8},{24,16},{9,1},{17,9},{25,17},{10,2},{18,10},{26,18},{... | collective-permute-start | bytes 786440 | tf_op jit(solution)/shard_map/ppermute | solution.py:188
  65.8 9.6 %collective-permute-start.13 = (s32[2,2,16,256]{3,2,1,0:T(8,128)S(1)}, s32[2,2,16,256]{3,2,1,0:T(8,128)S(1)}, u32[]{:S(2)}, u32[]{:S(2)}) collective-permute-start(s32[2,2,16,256]{3,2,1,0:T(8,128)S(1)} %copy-done.28), channel_id=1, source_target_pairs={{0,24},{8,16},{16,8},{24,0},{1,25},{9,17},{17,9},{25,1},{2,26},{10... | collective-permute-start | bytes 196616 | tf_op jit(solution)/shard_map/ppermute | solution.py:154
  75.6 5.1 %collective-permute-start.14 = (bf16[2,128,256]{2,1,0:T(8,128)(2,1)S(1)}, bf16[2,128,256]{2,1,0:T(8,128)(2,1)S(1)}, u32[]{:S(2)}, u32[]{:S(2)}) collective-permute-start(bf16[2,128,256]{2,1,0:T(8,128)(2,1)S(1)} %get-tuple-element.36), channel_id=1, source_target_pairs={{0,1},{1,2},{2,3},{3,4},{4,5},{5,6},{6,7},{8,9},{9,10},{10,11},{11... | collective-permute-start | bytes 393224 | tf_op jit(solution)/shard_map/ppermute | solution.py:149
  85.3 7.0 %collective-permute-start.16 = (bf16[2,128,256]{2,1,0:T(8,128)(2,1)S(1)}, bf16[2,128,256]{2,1,0:T(8,128)(2,1)S(1)}, u32[]{:S(2)}, u32[]{:S(2)}) collective-permute-start(bf16[2,128,256]{2,1,0:T(8,128)(2,1)S(1)} %get-tuple-element.34), channel_id=1, source_target_pairs={{0,1},{1,2},{2,3},{3,4},{4,5},{5,6},{6,7},{8,9},{9,10},{10,11},{11... | collective-permute-start | bytes 393224 | tf_op jit(solution)/shard_map/ppermute | solution.py:149
  92.2 8.3 %collective-permute-start.19 = (s32[2,2,16,256]{3,2,1,0:T(8,128)S(1)}, s32[2,2,16,256]{3,2,1,0:T(8,128)S(1)}, u32[]{:S(2)}, u32[]{:S(2)}) collective-permute-start(s32[2,2,16,256]{3,2,1,0:T(8,128)S(1)} %copy-done.27), channel_id=1, source_target_pairs={{0,24},{8,16},{16,8},{24,0},{1,25},{9,17},{17,9},{25,1},{2,26},{10... | collective-permute-start | bytes 196616 | tf_op jit(solution)/shard_map/ppermute | solution.py:154
  95.0 8.5 %collective-permute-start.18 = (bf16[2,2,128,256]{3,2,1,0:T(8,128)(2,1)S(1)}, bf16[2,2,128,256]{3,2,1,0:T(8,128)(2,1)S(1)}, u32[]{:S(2)}, u32[]{:S(2)}) collective-permute-start(bf16[2,2,128,256]{3,2,1,0:T(8,128)(2,1)S(1)} %shard_map.85), channel_id=1, source_target_pairs={{8,0},{16,8},{24,16},{9,1},{17,9},{25,17},{10,2},{18,10},{26,18},{... | collective-permute-start | bytes 786440 | tf_op jit(solution)/shard_map/ppermute | solution.py:188
  96.4 20.4 %collective-permute-start.29 = (bf16[4,2,128,256]{3,2,1,0:T(8,128)(2,1)S(1)}, bf16[4,2,128,256]{3,2,1,0:T(8,128)(2,1)S(1)}, u32[]{:S(2)}, u32[]{:S(2)}) collective-permute-start(bf16[4,2,128,256]{3,2,1,0:T(8,128)(2,1)S(1)} %get-tuple-element.8), channel_id=1, source_target_pairs={{0,24},{8,16},{16,8},{24,0},{1,25},{9,17},{17,9},{25,1},{2,26},{10... | collective-permute-start | bytes 1572872 | tf_op jit(solution)/shard_map/ppermute | solution.py:154
  103.7 13.1 %collective-permute-start.20 = (bf16[2,128,256]{2,1,0:T(8,128)(2,1)S(1)}, bf16[2,128,256]{2,1,0:T(8,128)(2,1)S(1)}, u32[]{:S(2)}, u32[]{:S(2)}) collective-permute-start(bf16[2,128,256]{2,1,0:T(8,128)(2,1)S(1)} %get-tuple-element.32), channel_id=1, source_target_pairs={{0,1},{1,2},{2,3},{3,4},{4,5},{5,6},{6,7},{8,9},{9,10},{10,11},{11... | collective-permute-start | bytes 393224 | tf_op jit(solution)/shard_map/ppermute | solution.py:149
  122.0 70.2 %reduce-scatter.3.cloned.1.call-start = ((), (), s32[]{:S(2)}) async-start(), calls=%async_computation.2 | async-start | bytes 1327104 | tf_op jit(solution)/shard_map/reduce_scatter | solution.py:206
  123.4 15.1 %collective-permute-start.28 = (bf16[4,2,128,256]{3,2,1,0:T(8,128)(2,1)S(1)}, bf16[4,2,128,256]{3,2,1,0:T(8,128)(2,1)S(1)}, u32[]{:S(2)}, u32[]{:S(2)}) collective-permute-start(bf16[4,2,128,256]{3,2,1,0:T(8,128)(2,1)S(1)} %get-tuple-element.6), channel_id=1, source_target_pairs={{0,24},{8,16},{16,8},{24,0},{1,25},{9,17},{17,9},{25,1},{2,26},{10... | collective-permute-start | bytes 1572872 | tf_op jit(solution)/shard_map/ppermute | solution.py:154
  124.5 14.1 %collective-permute-start.22 = (bf16[2,128,256]{2,1,0:T(8,128)(2,1)S(1)}, bf16[2,128,256]{2,1,0:T(8,128)(2,1)S(1)}, u32[]{:S(2)}, u32[]{:S(2)}) collective-permute-start(bf16[2,128,256]{2,1,0:T(8,128)(2,1)S(1)} %get-tuple-element.30), channel_id=1, source_target_pairs={{0,1},{1,2},{2,3},{3,4},{4,5},{5,6},{6,7},{8,9},{9,10},{10,11},{11... | collective-permute-start | bytes 393224 | tf_op jit(solution)/shard_map/ppermute | solution.py:149
  128.0 10.5 %collective-permute-start.23 = (bf16[2,128,256]{2,1,0:T(8,128)(2,1)S(1)}, bf16[2,128,256]{2,1,0:T(8,128)(2,1)S(1)}, u32[]{:S(2)}, u32[]{:S(2)}) collective-permute-start(bf16[2,128,256]{2,1,0:T(8,128)(2,1)S(1)} %get-tuple-element.29), channel_id=1, source_target_pairs={{1,0},{2,1},{3,2},{4,3},{5,4},{6,5},{7,6},{9,8},{10,9},{11,10},{12... | collective-permute-start | bytes 393224 | tf_op jit(solution)/shard_map/ppermute | solution.py:149
  142.5 7.3 %collective-permute-start.24 = (bf16[2,128,256]{2,1,0:T(8,128)(2,1)S(1)}, bf16[2,128,256]{2,1,0:T(8,128)(2,1)S(1)}, u32[]{:S(2)}, u32[]{:S(2)}) collective-permute-start(bf16[2,128,256]{2,1,0:T(8,128)(2,1)S(1)} %get-tuple-element.22), channel_id=1, source_target_pairs={{0,24},{8,16},{16,8},{24,0},{1,25},{9,17},{17,9},{25,1},{2,26},{10... | collective-permute-start | bytes 393224 | tf_op jit(solution)/shard_map/ppermute | solution.py:154
  142.6 10.0 %collective-permute-start.25 = (bf16[2,128,256]{2,1,0:T(8,128)(2,1)S(1)}, bf16[2,128,256]{2,1,0:T(8,128)(2,1)S(1)}, u32[]{:S(2)}, u32[]{:S(2)}) collective-permute-start(bf16[2,128,256]{2,1,0:T(8,128)(2,1)S(1)} %get-tuple-element.24), channel_id=1, source_target_pairs={{0,24},{8,16},{16,8},{24,0},{1,25},{9,17},{17,9},{25,1},{2,26},{10... | collective-permute-start | bytes 393224 | tf_op jit(solution)/shard_map/ppermute | solution.py:154
  145.6 9.9 %collective-permute-start.26 = (bf16[2,128,256]{2,1,0:T(8,128)(2,1)S(1)}, bf16[2,128,256]{2,1,0:T(8,128)(2,1)S(1)}, u32[]{:S(2)}, u32[]{:S(2)}) collective-permute-start(bf16[2,128,256]{2,1,0:T(8,128)(2,1)S(1)} %get-tuple-element.26), channel_id=1, source_target_pairs={{0,24},{8,16},{16,8},{24,0},{1,25},{9,17},{17,9},{25,1},{2,26},{10... | collective-permute-start | bytes 393224 | tf_op jit(solution)/shard_map/ppermute | solution.py:154
  146.5 11.3 %collective-permute-start.27 = (bf16[2,128,256]{2,1,0:T(8,128)(2,1)S(1)}, bf16[2,128,256]{2,1,0:T(8,128)(2,1)S(1)}, u32[]{:S(2)}, u32[]{:S(2)}) collective-permute-start(bf16[2,128,256]{2,1,0:T(8,128)(2,1)S(1)} %get-tuple-element.28), channel_id=1, source_target_pairs={{0,24},{8,16},{16,8},{24,0},{1,25},{9,17},{17,9},{25,1},{2,26},{10... | collective-permute-start | bytes 393224 | tf_op jit(solution)/shard_map/ppermute | solution.py:154
  (37 other events, 286.9 us)
Sparse Core Ops, SparseCore 0:
  122.1 36.3 reduce-scatter.4
  160.8 31.3 reduce-scatter.2
where the time goes:
time: 202 us; the launch traced here: 201 us
  waiting for transfers between devices  89.3 us (44%)
  starting transfers between devices  71.3 us (35%)
  between operations  14.9 us (7%)
  Pallas kernels  14.7 us (7%)
  local copies, waits for them, and re-layouts  6.73 us (3%)
  other arithmetic  3.98 us (2%)
    ppermute x8, starting transfers between devices, edges(): lax.ppermute(x[:, -1], 'row', down)  37.6 us
    ppermute x11, waiting for transfers between devices, mirrored(): return lax.ppermute(x, 'section', [(i, size - 1 - i) for i in range(size)])  35.1 us
    reduce_scatter x2, waiting for transfers between devices, scattered(): lax.psum_scatter(x, 'row', scatter_dimension=0, tiled=True).astype(F32)  32.3 us
    ppermute x11, starting transfers between devices, mirrored(): return lax.ppermute(x, 'section', [(i, size - 1 - i) for i in range(size)])  19.2 us
    pallas_call x14, Pallas kernels, call(): pl.pallas_call(kernel, out_shape=out_shape, in_specs=specs or [VMEM] * le...  14.7 us
    ppermute x8, waiting for transfers between devices, edges(): lax.ppermute(x[:, 0], 'row', up)  13.4 us
    ppermute x8, starting transfers between devices, edges(): lax.ppermute(x[:, 0], 'row', up)  10.5 us
    ppermute x3, waiting for transfers between devices, per_device(): handed = lax.ppermute(produced, 'section', below)  8.49 us
  transfers between devices with their start and end apart: 32, of which 19 were waited for; matrix products, arithmetic and copies ran while one was open for 3% of the time, Pallas kernels for 4%

commit v1 on v0

v1 whole, which is shorter than its diff:
```python
import math

import jax
import jax.numpy as jnp
from jax import lax
from jax.experimental import pallas as pl
from jax.experimental.pallas import tpu as pltpu
from jax.sharding import PartitionSpec as P

F32 = jnp.float32
BF16 = jnp.bfloat16
VMEM = pl.BlockSpec(memory_space=pltpu.VMEM)


def gate_of(words):
    groups, channels = words.shape
    bit = lax.broadcasted_iota(jnp.int32, (8, channels), 0)
    pieces = [
        jnp.bitwise_and(
            jnp.right_shift(jnp.broadcast_to(words[j : j + 1, :], (8, channels)), bit), 1
        )
        for j in range(groups)
    ]
    return jnp.concatenate(pieces, axis=0).astype(F32)


def shifted(x, step):
    cols = x.shape[0]
    rolled = pltpu.roll(x, (-step) % cols, 0)
    at = lax.broadcasted_iota(jnp.int32, x.shape, 0)
    edge = cols - 1 if step == 1 else 0
    return jnp.where(at == edge, 0.0, rolled)


def transposed(core_ref, above_ref, below_ref, w_ref, w_at):
    replicas, rows, cols, channels = core_ref.shape
    padded = [
        [above_ref[r]] + [core_ref[r, i] for i in range(rows)] + [below_ref[r]]
        for r in range(replicas)
    ]
    lhs = jnp.concatenate(
        [
            jnp.concatenate(
                [padded[r][i - u + 2] for r in range(replicas) for i in range(rows)], axis=0
            )
            for u in range(3)
        ],
        axis=1,
    )
    parts = []
    for v in range(3):
        rhs = jnp.concatenate(
            [w_ref[0, w_at, pl.ds((u * 3 + v) * channels, channels), :] for u in range(3)], axis=1
        )
        parts.append(
            lax.dot_general(lhs, rhs, (((1,), (1,)), ((), ())), preferred_element_type=F32)
        )
    out = []
    for n in range(replicas * rows):
        low, mid, high = (part[n * cols : (n + 1) * cols] for part in parts)
        out.append(shifted(low, 1) + mid + shifted(high, -1))
    return out


MESH = pl.DeviceIdType.MESH


def relay_kernel(
    flight_ref, fresh_ref, inputs_ref, hidden_ref, masks_ref, w_ref,
    grads_ref, wgrads_ref,
    flight_in, words_in, inputs_in, hidden_in, handed, produced,
    g_ref, above, below, total, term, pair_in, pair_sum, chip_in, xt, yt,
    flight_sem, words_sem, saved_sem, hand_sem, back_sem, up_sem, down_sem, pair_sem, chip_sem,
):
    sections, bands = lax.axis_size("section"), lax.axis_size("row")
    sec, row = lax.axis_index("section"), lax.axis_index("row")
    ticks, _, rows, cols, channels = inputs_ref.shape[1:]
    chips = bands // 2
    chip, core = row // 2, row % 2
    mirror = sections - 1 - sec
    share = 9 * channels // bands
    scale = 1.0 / math.sqrt(2 * ticks * rows * bands * cols)

    above[...] = jnp.zeros_like(above)
    below[...] = jnp.zeros_like(below)
    barrier = pltpu.get_barrier_semaphore()
    peers = [(sec, (row + d) % bands) for d in range(1, bands)]
    peers += [(mirror, row), ((sec + 1) % sections, row), ((sec + sections - 1) % sections, row)]
    for peer in peers:
        pl.semaphore_signal(barrier, inc=1, device_id=peer, device_id_type=MESH)
    pl.semaphore_wait(barrier, len(peers))

    waits = []

    def copy(source, target, sems, device):
        return pltpu.make_async_remote_copy(
            src_ref=source, dst_ref=target, send_sem=sems.at[0], recv_sem=sems.at[1],
            device_id=device, device_id_type=MESH,
        )

    def send(c, when=None):
        if when is None:
            c.start()
        else:
            pl.when(when)(c.start)
        waits.append((c, when))
        return c

    def arrive(c, when=None):
        if when is None:
            c.wait_recv()
        else:
            pl.when(when)(c.wait_recv)

    other = (mirror, row)
    flight_copy = send(copy(flight_ref.at[1, 0], flight_in, flight_sem, other))
    words_copies = [
        copy(masks_ref.at[1, t, 0], words_in.at[t], words_sem.at[t], other) for t in range(ticks)
    ]
    hidden_copies = [
        copy(hidden_ref.at[1, t, 0], hidden_in.at[t], saved_sem.at[1, t], other)
        for t in range(ticks)
    ]
    inputs_copies = [
        copy(inputs_ref.at[1, t, 0], inputs_in.at[t], saved_sem.at[0, t], other)
        for t in range(ticks)
    ]
    send(words_copies[0])
    queue = [
        words_copies[1:2] + hidden_copies[:2],
        words_copies[2:3] + hidden_copies[2:] + inputs_copies[:1],
        words_copies[3:] + inputs_copies[1:3],
        inputs_copies[3:],
    ]

    has_above, has_below = row > 0, row < bands - 1
    up_peer = (sec, jnp.maximum(row - 1, 0))
    down_peer = (sec, jnp.minimum(row + 1, bands - 1))

    def words(r, t, k, i):
        return masks_ref[0, t, 0, k, i] if r == 0 else words_in[t, k, i]

    def exchange(k, t):
        pairs = []
        for r in range(2):
            up = copy(g_ref.at[k, t, r, 0], below.at[k, t, r], up_sem.at[k, t, r], up_peer)
            down = copy(
                g_ref.at[k, t, r, rows - 1], above.at[k, t, r], down_sem.at[k, t, r], down_peer
            )
            send(up, has_above)
            send(down, has_below)
            pairs.append((up, down))
        return pairs

    def arrived(pairs):
        for up, down in pairs:
            arrive(up, has_below)
            arrive(down, has_above)

    def gate(t, state):
        for r in range(2):
            for i in range(rows):
                value = state(r, i).astype(F32) * gate_of(words(r, t, 1, i))
                g_ref[1, t, r, i] = value.astype(BF16)

    def add_terms(k, t):
        own, far = (inputs_ref, inputs_in) if k == 0 else (hidden_ref, hidden_in)
        for r in range(2):
            for i in range(rows):
                at = (r * rows + i) * cols
                x = own[0, t, 0, i] if r == 0 else far[t, i]
                xt[:, at : at + cols] = x.T
        for v in range(3):
            for r in range(2):
                lines = [above[k, t, r]] + [g_ref[k, t, r, i] for i in range(rows)] + [below[k, t, r]]
                for n, line in enumerate(lines):
                    if v != 1:
                        line = shifted(line.astype(F32), 1 - v).astype(BF16)
                    for u in range(3):
                        i = n + u - 2
                        if 0 <= i < rows:
                            at = (r * rows + i) * cols
                            yt[at : at + cols, u * channels : (u + 1) * channels] = line
            value = jnp.dot(xt[...], yt[...], preferred_element_type=F32)
            for u in range(3):
                part = value[:, u * channels : (u + 1) * channels]
                first = (u * 3 + v) * channels
                where = pl.ds(first, channels)
                if t > 0:
                    part = part + total[k, where, :]
                if t < ticks - 1:
                    total[k, where, :] = part
                    continue
                at = first
                while at < first + channels:
                    piece, offset = at // share, at % share
                    length = min(share - offset, first + channels - at)
                    term[k, piece, offset : offset + length, :] = part[
                        at - first : at - first + length
                    ].astype(BF16)
                    at += length

    def pair_start(k):
        copies = []
        for z in range(chips):
            copies.append(
                send(
                    copy(term.at[k, 2 * z + 1 - core], pair_in.at[k, z], pair_sem.at[k, z],
                         (sec, row + 1 - 2 * core))
                )
            )
        return copies

    def chip_start(k, pairs):
        for c in pairs:
            c.wait_recv()
        copies = []
        for d in range(1, chips):
            z = (chip + d) % chips
            value = term[k, 2 * z + core].astype(F32) + pair_in[k, z].astype(F32)
            pair_sum[k, d - 1] = value.astype(BF16)
            copies.append(
                send(
                    copy(pair_sum.at[k, d - 1], chip_in.at[k, d - 1], chip_sem.at[k, d - 1],
                         (sec, 2 * z + core))
                )
            )
        return copies

    def finish(k, copies):
        value = term[k, 2 * chip + core].astype(F32) + pair_in[k, chip].astype(F32)
        for d, c in enumerate(copies):
            c.wait_recv()
            value = value + chip_in[k, d].astype(F32)
        wgrads_ref[0, k] = value * scale

    is_last = sec == sections - 1
    hand = None
    backs = []
    for t in range(ticks):
        if t == 0:
            flight_copy.wait_recv()
            words_copies[0].wait_recv()
            gate(t, lambda r, i: flight_ref[0, 0, i] if r == 0 else flight_in[i])
        else:
            words_copies[t].wait_recv()
            arrive(hand, jnp.logical_not(is_last))

            @pl.when(is_last)
            def _():
                gate(t, lambda r, i: fresh_ref[r, t - 1, i])

            @pl.when(jnp.logical_not(is_last))
            def _():
                gate(t, lambda r, i: handed[t - 1, r, i])

        pairs = exchange(1, t)
        for c in queue[t] if t < len(queue) else []:
            send(c)
        arrived(pairs)
        back = transposed(g_ref.at[1, t], above.at[1, t], below.at[1, t], w_ref, 1)
        for r in range(2):
            for i in range(rows):
                g_ref[0, t, r, i] = (back[r * rows + i] * gate_of(words(r, t, 0, i))).astype(BF16)
        pairs = exchange(0, t)
        hidden_copies[t].wait_recv()
        if t == ticks - 1:
            add_terms(1, t)
            second = pair_start(1)
        arrived(pairs)
        back = transposed(g_ref.at[0, t], above.at[0, t], below.at[0, t], w_ref, 0)
        for r in range(2):
            for i in range(rows):
                value = (g_ref[1, t, r, i].astype(F32) + back[r * rows + i]).astype(BF16)
                produced[t, r, i] = value
                if r == 0:
                    grads_ref[0, t, 0, i] = value
        if t < ticks - 1:
            hand = copy(produced.at[t], handed.at[t], hand_sem.at[t], (jnp.maximum(sec - 1, 0), row))
            send(hand, sec > 0)
        backs.append(send(copy(produced.at[t, 1], grads_ref.at[1, t, 0], back_sem.at[t], other)))
        if t < ticks - 1:
            add_terms(1, t)
            if t > 0:
                inputs_copies[t - 1].wait_recv()
                add_terms(0, t - 1)
    second = chip_start(1, second)
    for t in range(ticks - 2, ticks):
        inputs_copies[t].wait_recv()
        add_terms(0, t)
    first = pair_start(0)
    first = chip_start(0, first)
    finish(1, second)
    finish(0, first)
    for c in backs:
        c.wait_recv()
    for c, when in waits:
        if when is None:
            c.wait_send()
        else:
            pl.when(when)(c.wait_send)


def per_device(in_flight, fresh, saved_inputs, saved_hidden, masks, weights):
    bands = lax.axis_size("row")
    ticks = saved_inputs.shape[1]
    rows, cols, channels = saved_inputs.shape[3:]
    chips, share = bands // 2, 9 * channels // bands
    span = 2 * rows * cols
    line = (rows, cols, channels)
    dma = pltpu.SemaphoreType.DMA
    scratch = [
        pltpu.VMEM(line, BF16),
        pltpu.VMEM((ticks,) + masks.shape[3:], jnp.int32),
        pltpu.VMEM((ticks,) + line, BF16),
        pltpu.VMEM((ticks,) + line, BF16),
        pltpu.VMEM((ticks - 1, 2) + line, BF16),
        pltpu.VMEM((ticks, 2) + line, BF16),
        pltpu.VMEM((2, ticks, 2) + line, BF16),
        pltpu.VMEM((2, ticks, 2) + line[1:], BF16),
        pltpu.VMEM((2, ticks, 2) + line[1:], BF16),
        pltpu.VMEM((2, 9 * channels, channels), F32),
        pltpu.VMEM((2, bands, share, channels), BF16),
        pltpu.VMEM((2, chips, share, channels), BF16),
        pltpu.VMEM((2, chips - 1, share, channels), BF16),
        pltpu.VMEM((2, chips - 1, share, channels), BF16),
        pltpu.VMEM((channels, span), BF16),
        pltpu.VMEM((span, 3 * channels), BF16),
        dma((2,)), dma((ticks, 2)), dma((2, ticks, 2)), dma((ticks - 1, 2)), dma((ticks, 2)),
        dma((2, ticks, 2, 2)), dma((2, ticks, 2, 2)), dma((2, chips, 2)), dma((2, chips - 1, 2)),
    ]
    return pl.pallas_call(
        relay_kernel,
        out_shape=(
            jax.ShapeDtypeStruct(saved_inputs.shape, BF16),
            jax.ShapeDtypeStruct((1, 2, share, channels), F32),
        ),
        in_specs=[VMEM] * 6,
        out_specs=(VMEM, VMEM),
        scratch_shapes=scratch,
        compiler_params=pltpu.CompilerParams(
            collective_id=0, has_side_effects=True, vmem_limit_bytes=48 << 20
        ),
    )(in_flight, fresh, saved_inputs, saved_hidden, masks, weights)


def solution(mesh):
    return jax.shard_map(
        per_device,
        mesh=mesh,
        in_specs=(
            P(None, "section", "row", None, None),
            P(None, None, "row", None, None),
            P(None, None, "section", "row", None, None),
            P(None, None, "section", "row", None, None),
            P(None, None, "section", None, "row", None, None),
            P("section", None, None, None),
        ),
        out_specs=(P(None, None, "section", "row", None, None), P("section", None, "row", None)),
        check_vma=False,
    )
```

time: 202 us -> 111 us (0.55)
  the two profiles are of different devices: /device:TPU:0 before, /device:TPU:24 now
where the time goes in v1:
time: 111 us
  Pallas kernels  103 us (93%)
  local copies, waits for them, and re-layouts  7.35 us (7%)
    pallas_call x1, Pallas kernels, per_device(): pl.pallas_call(relay_kernel, out_shape=(jax.ShapeDtypeStruct(saved_inputs...  103 us
    unnamed x12, local copies, waits for them, and re-layouts  7.35 us

profile of v1, /device:TPU:24, one launch (start us, length us, event | category | flops | bytes accessed | tf_op | source)
XLA Modules:
  0.0 111.1 jit_solution(9478405184397023473)
XLA Ops:
  0.6 0.0 copy-start
  0.6 1.2 %copy-done = bf16[2,4,1,2,128,256]{5,4,3,2,1,0:T(8,128)(2,1)S(1)} copy-done((bf16[2,4,1,2,128,256]{5,4,3,2,1,0:T(8,128)(2,1)S(1)}, bf16[2,4,1,2,128,256]{5,4,3,2,1,0:T(8,128)(2,1)}, u32[]{:S(2)}) %copy-start) | copy-done | bytes 1048600
  1.9 0.0 copy-start.1
  1.9 1.2 %copy-done.1 = bf16[2,4,1,2,128,256]{5,4,3,2,1,0:T(8,128)(2,1)S(1)} copy-done((bf16[2,4,1,2,128,256]{5,4,3,2,1,0:T(8,128)(2,1)S(1)}, bf16[2,4,1,2,128,256]{5,4,3,2,1,0:T(8,128)(2,1)}, u32[]{:S(2)}) %copy-start.1) | copy-done | bytes 1048600
  3.1 0.0 copy-start.2
  3.1 1.1 %copy-done.2 = bf16[2,3,2,128,256]{4,3,2,1,0:T(8,128)(2,1)S(1)} copy-done((bf16[2,3,2,128,256]{4,3,2,1,0:T(8,128)(2,1)S(1)}, bf16[2,3,2,128,256]{4,3,2,1,0:T(8,128)(2,1)}, u32[]{:S(2)}) %copy-start.2) | copy-done | bytes 786456
  4.2 0.0 copy-start.3
  4.2 1.0 copy-done.3
  5.3 0.0 copy-start.4
  5.3 0.9 copy-done.4
  6.2 103.1 %shard_map.77 = (bf16[2,4,1,2,128,256]{5,4,3,2,1,0:T(8,128)(2,1)S(1)}, f32[1,2,288,256]{3,2,1,0:T(8,128)S(1)}) custom-call(bf16[2,1,2,128,256]{4,3,2,1,0:T(8,128)(2,1)S(1)} %copy-done.4, bf16[2,3,2,128,256]{4,3,2,1,0:T(8,128)(2,1)S(1)} %copy-done.2, bf16[2,4,1,2,128,256]{5,4,3,2,1,0:T(8,128)(2,1)S(1)} %copy-done, ...), custom_call_target="tpu_custom_call" | custom-call | tf_op jit(solution)/shard_map/pallas_call | solution.py:332
  109.3 1.0 copy.10
  110.3 0.8 copy.11
Async XLA Ops:
  0.6 1.2 %copy-start = (bf16[2,4,1,2,128,256]{5,4,3,2,1,0:T(8,128)(2,1)S(1)}, bf16[2,4,1,2,128,256]{5,4,3,2,1,0:T(8,128)(2,1)}, u32[]{:S(2)}) copy-start(bf16[2,4,1,2,128,256]{5,4,3,2,1,0:T(8,128)(2,1)} %inputs_ref.1) | copy-start | bytes 3145732
  1.9 1.2 %copy-start.1 = (bf16[2,4,1,2,128,256]{5,4,3,2,1,0:T(8,128)(2,1)S(1)}, bf16[2,4,1,2,128,256]{5,4,3,2,1,0:T(8,128)(2,1)}, u32[]{:S(2)}) copy-start(bf16[2,4,1,2,128,256]{5,4,3,2,1,0:T(8,128)(2,1)} %hidden_ref.1) | copy-start | bytes 3145732
  3.1 1.1 %copy-start.2 = (bf16[2,3,2,128,256]{4,3,2,1,0:T(8,128)(2,1)S(1)}, bf16[2,3,2,128,256]{4,3,2,1,0:T(8,128)(2,1)}, u32[]{:S(2)}) copy-start(bf16[2,3,2,128,256]{4,3,2,1,0:T(8,128)(2,1)} %fresh_ref.1) | copy-start | bytes 2359300
  4.2 1.0 copy-start.3
  5.3 0.9 copy-start.4

commit v2 on v1

--- a/solution.py
+++ b/solution.py
@@ -32,31 +32,23 @@
     return jnp.where(at == edge, 0.0, rolled)
 
 
-def transposed(core_ref, above_ref, below_ref, w_ref, w_at):
-    replicas, rows, cols, channels = core_ref.shape
-    padded = [
-        [above_ref[r]] + [core_ref[r, i] for i in range(rows)] + [below_ref[r]]
-        for r in range(replicas)
-    ]
+def transposed(core_ref, above_ref, below_ref, w_ref):
+    rows, cols, channels = core_ref.shape
+    padded = [above_ref[...]] + [core_ref[i] for i in range(rows)] + [below_ref[...]]
     lhs = jnp.concatenate(
-        [
-            jnp.concatenate(
-                [padded[r][i - u + 2] for r in range(replicas) for i in range(rows)], axis=0
-            )
-            for u in range(3)
-        ],
+        [jnp.concatenate([padded[i - u + 2] for i in range(rows)], axis=0) for u in range(3)],
         axis=1,
     )
     parts = []
     for v in range(3):
         rhs = jnp.concatenate(
-            [w_ref[0, w_at, pl.ds((u * 3 + v) * channels, channels), :] for u in range(3)], axis=1
+            [w_ref[pl.ds((u * 3 + v) * channels, channels), :] for u in range(3)], axis=1
         )
         parts.append(
             lax.dot_general(lhs, rhs, (((1,), (1,)), ((), ())), preferred_element_type=F32)
         )
     out = []
-    for n in range(replicas * rows):
+    for n in range(rows):
         low, mid, high = (part[n * cols : (n + 1) * cols] for part in parts)
         out.append(shifted(low, 1) + mid + shifted(high, -1))
     return out
@@ -68,6 +60,7 @@
 def relay_kernel(
     flight_ref, fresh_ref, inputs_ref, hidden_ref, masks_ref, w_ref,
     grads_ref, wgrads_ref,
+    flight_own, fresh_own, inputs_own, hidden_own, words_own, w_own, load_sem,
     flight_in, words_in, inputs_in, hidden_in, handed, produced,
     g_ref, above, below, total, term, pair_in, pair_sum, chip_in, xt, yt,
     flight_sem, words_sem, saved_sem, hand_sem, back_sem, up_sem, down_sem, pair_sem, chip_sem,
@@ -81,6 +74,22 @@
     share = 9 * channels // bands
     scale = 1.0 / math.sqrt(2 * ticks * rows * bands * cols)
 
+    loads = [
+        pltpu.make_async_copy(source, target, load_sem.at[n])
+        for n, (source, target) in enumerate(
+            [
+                (flight_ref.at[0, 0], flight_own),
+                (masks_ref.at[0, :, 0], words_own),
+                (w_ref.at[0, 1], w_own.at[1]),
+                (w_ref.at[0, 0], w_own.at[0]),
+                (fresh_ref, fresh_own),
+                (hidden_ref.at[0, :, 0], hidden_own),
+                (inputs_ref.at[0, :, 0], inputs_own),
+            ]
+        )
+    ]
+    for load in loads:
+        load.start()
     above[...] = jnp.zeros_like(above)
     below[...] = jnp.zeros_like(below)
     barrier = pltpu.get_barrier_semaphore()
@@ -127,10 +136,9 @@
     ]
     send(words_copies[0])
     queue = [
-        words_copies[1:2] + hidden_copies[:2],
-        words_copies[2:3] + hidden_copies[2:] + inputs_copies[:1],
-        words_copies[3:] + inputs_copies[1:3],
-        inputs_copies[3:],
+        words_copies[1:2] + hidden_copies[:1] + inputs_copies[:1] + hidden_copies[1:2],
+        words_copies[2:3] + inputs_copies[1:2] + hidden_copies[2:3],
+        words_copies[3:] + inputs_copies[2:3] + hidden_copies[3:] + inputs_copies[3:],
     ]
 
     has_above, has_below = row > 0, row < bands - 1
@@ -138,37 +146,29 @@
     down_peer = (sec, jnp.minimum(row + 1, bands - 1))
 
     def words(r, t, k, i):
-        return masks_ref[0, t, 0, k, i] if r == 0 else words_in[t, k, i]
-
-    def exchange(k, t):
-        pairs = []
-        for r in range(2):
-            up = copy(g_ref.at[k, t, r, 0], below.at[k, t, r], up_sem.at[k, t, r], up_peer)
-            down = copy(
-                g_ref.at[k, t, r, rows - 1], above.at[k, t, r], down_sem.at[k, t, r], down_peer
-            )
-            send(up, has_above)
-            send(down, has_below)
-            pairs.append((up, down))
-        return pairs
-
-    def arrived(pairs):
-        for up, down in pairs:
-            arrive(up, has_below)
-            arrive(down, has_above)
-
-    def gate(t, state):
-        for r in range(2):
-            for i in range(rows):
-                value = state(r, i).astype(F32) * gate_of(words(r, t, 1, i))
-                g_ref[1, t, r, i] = value.astype(BF16)
+        return words_own[t, k, i] if r == 0 else words_in[t, k, i]
+
+    def exchange(k, t, r):
+        up = copy(g_ref.at[k, t, r, 0], below.at[k, t, r], up_sem.at[k, t, r], up_peer)
+        down = copy(g_ref.at[k, t, r, rows - 1], above.at[k, t, r], down_sem.at[k, t, r], down_peer)
+        send(up, has_above)
+        send(down, has_below)
+        return up, down
+
+    def arrived(pair):
+        arrive(pair[0], has_below)
+        arrive(pair[1], has_above)
+
+    def gate(t, r, state):
+        for i in range(rows):
+            g_ref[1, t, r, i] = (state(i).astype(F32) * gate_of(words(r, t, 1, i))).astype(BF16)
 
     def add_terms(k, t):
-        own, far = (inputs_ref, inputs_in) if k == 0 else (hidden_ref, hidden_in)
+        own, far = (inputs_own, inputs_in) if k == 0 else (hidden_own, hidden_in)
         for r in range(2):
             for i in range(rows):
                 at = (r * rows + i) * cols
-                x = own[0, t, 0, i] if r == 0 else far[t, i]
+                x = (own if r == 0 else far)[t, i]
                 xt[:, at : at + cols] = x.T
         for v in range(3):
             for r in range(2):
@@ -235,59 +235,81 @@
         wgrads_ref[0, k] = value * scale
 
     is_last = sec == sections - 1
-    hand = None
+    hands = [None, None]
     backs = []
+    loads[0].wait()
+    loads[1].wait()
     for t in range(ticks):
+        pairs = []
+        for r in range(2):
+            if t == 0:
+                if r == 1:
+                    flight_copy.wait_recv()
+                    words_copies[0].wait_recv()
+                gate(t, r, lambda i: flight_own[i] if r == 0 else flight_in[i])
+            else:
+                if r == 1:
+                    words_copies[t].wait_recv()
+                elif t == 1:
+                    loads[4].wait()
+
+                @pl.when(is_last)
+                def _():
+                    gate(t, r, lambda i: fresh_own[r, t - 1, i])
+
+                @pl.when(jnp.logical_not(is_last))
+                def _():
+                    hands[r].wait_recv()
+                    gate(t, r, lambda i: handed[t - 1, r, i])
+
+            pairs.append(exchange(1, t, r))
+            if r == 0:
+                for c in queue[t] if t < len(queue) else []:
+                    send(c)
+            if r == 0 and t > 0:
+                inputs_copies[t - 1].wait_recv()
+                if t == 1:
+                    loads[6].wait()
+                add_terms(0, t - 1)
+        for r in range(2):
+            arrived(pairs[r])
+            if t == 0 and r == 0:
+                loads[2].wait()
+            band = g_ref.at[1, t, r]
+            back = transposed(band, above.at[1, t, r], below.at[1, t, r], w_own.at[1])
+            for i in range(rows):
+                g_ref[0, t, r, i] = (back[i] * gate_of(words(r, t, 0, i))).astype(BF16)
+            pairs[r] = exchange(0, t, r)
         if t == 0:
-            flight_copy.wait_recv()
-            words_copies[0].wait_recv()
-            gate(t, lambda r, i: flight_ref[0, 0, i] if r == 0 else flight_in[i])
-        else:
-            words_copies[t].wait_recv()
-            arrive(hand, jnp.logical_not(is_last))
-
-            @pl.when(is_last)
-            def _():
-                gate(t, lambda r, i: fresh_ref[r, t - 1, i])
-
-            @pl.when(jnp.logical_not(is_last))
-            def _():
-                gate(t, lambda r, i: handed[t - 1, r, i])
-
-        pairs = exchange(1, t)
-        for c in queue[t] if t < len(queue) else []:
-            send(c)
-        arrived(pairs)
-        back = transposed(g_ref.at[1, t], above.at[1, t], below.at[1, t], w_ref, 1)
-        for r in range(2):
-            for i in range(rows):
-                g_ref[0, t, r, i] = (back[r * rows + i] * gate_of(words(r, t, 0, i))).astype(BF16)
-        pairs = exchange(0, t)
-        hidden_copies[t].wait_recv()
+            loads[3].wait()
         if t == ticks - 1:
+            hidden_copies[t].wait_recv()
             add_terms(1, t)
             second = pair_start(1)
-        arrived(pairs)
-        back = transposed(g_ref.at[0, t], above.at[0, t], below.at[0, t], w_ref, 0)
         for r in range(2):
+            arrived(pairs[r])
+            band = g_ref.at[0, t, r]
+            back = transposed(band, above.at[0, t, r], below.at[0, t, r], w_own.at[0])
             for i in range(rows):
-                value = (g_ref[1, t, r, i].astype(F32) + back[r * rows + i]).astype(BF16)
+                value = (g_ref[1, t, r, i].astype(F32) + back[i]).astype(BF16)
                 produced[t, r, i] = value
                 if r == 0:
                     grads_ref[0, t, 0, i] = value
-        if t < ticks - 1:
-            hand = copy(produced.at[t], handed.at[t], hand_sem.at[t], (jnp.maximum(sec - 1, 0), row))
-            send(hand, sec > 0)
+            if t < ticks - 1:
+                hands[r] = copy(
+                    produced.at[t, r], handed.at[t, r], hand_sem.at[t, r],
+                    (jnp.maximum(sec - 1, 0), row),
+                )
+                send(hands[r], sec > 0)
         backs.append(send(copy(produced.at[t, 1], grads_ref.at[1, t, 0], back_sem.at[t], other)))
         if t < ticks - 1:
+            hidden_copies[t].wait_recv()
+            if t == 0:
+                loads[5].wait()
             add_terms(1, t)
-            if t > 0:
-                inputs_copies[t - 1].wait_recv()
-                add_terms(0, t - 1)
     second = chip_start(1, second)
-    for t in range(ticks - 2, ticks):
-        inputs_copies[t].wait_recv()
-        add_terms(0, t)
+    inputs_copies[ticks - 1].wait_recv()
+    add_terms(0, ticks - 1)
     first = pair_start(0)
     first = chip_start(0, first)
     finish(1, second)
@@ -310,6 +332,13 @@
     line = (rows, cols, channels)
     dma = pltpu.SemaphoreType.DMA
     scratch = [
+        pltpu.VMEM(line, BF16),
+        pltpu.VMEM(fresh.shape, BF16),
+        pltpu.VMEM((ticks,) + line, BF16),
+        pltpu.VMEM((ticks,) + line, BF16),
+        pltpu.VMEM((ticks,) + masks.shape[3:], jnp.int32),
+        pltpu.VMEM(weights.shape[1:], BF16),
+        dma((7,)),
         pltpu.VMEM(line, BF16),
         pltpu.VMEM((ticks,) + masks.shape[3:], jnp.int32),
         pltpu.VMEM((ticks,) + line, BF16),
@@ -326,7 +355,7 @@
         pltpu.VMEM((2, chips - 1, share, channels), BF16),
         pltpu.VMEM((channels, span), BF16),
         pltpu.VMEM((span, 3 * channels), BF16),
-        dma((2,)), dma((ticks, 2)), dma((2, ticks, 2)), dma((ticks - 1, 2)), dma((ticks, 2)),
+        dma((2,)), dma((ticks, 2)), dma((2, ticks, 2)), dma((ticks - 1, 2, 2)), dma((ticks, 2)),
         dma((2, ticks, 2, 2)), dma((2, ticks, 2, 2)), dma((2, chips, 2)), dma((2, chips - 1, 2)),
     ]
     return pl.pallas_call(
@@ -335,7 +364,7 @@
             jax.ShapeDtypeStruct(saved_inputs.shape, BF16),
             jax.ShapeDtypeStruct((1, 2, share, channels), F32),
         ),
-        in_specs=[VMEM] * 6,
+        in_specs=[pl.BlockSpec(memory_space=pltpu.MemorySpace.HBM)] * 6,
         out_specs=(VMEM, VMEM),
         scratch_shapes=scratch,
         compiler_params=pltpu.CompilerParams(

time: 111 us -> 102 us (0.919)
  Pallas kernels: 103 us -> 93.8 us
    pallas_call x1, Pallas kernels: 103 us -> 93.8 us  [per_device(): pl.pallas_call(relay_kernel, out_shape=(jax.ShapeDtypeStruct(saved_inputs...]
where the time goes in v2:
time: 102 us
  Pallas kernels  93.8 us (92%)
  local copies, waits for them, and re-layouts  7.35 us (7%)
    pallas_call x1, Pallas kernels, per_device(): pl.pallas_call(relay_kernel, out_shape=(jax.ShapeDtypeStruct(saved_inputs...  93.8 us
    unnamed x12, local copies, waits for them, and re-layouts  7.35 us

profile of v2, /device:TPU:24, one launch (start us, length us, event | category | flops | bytes accessed | tf_op | source)
XLA Modules:
  0.0 101.8 jit_solution(17786931027039540076)
XLA Ops:
  0.6 0.0 copy-start
  0.6 1.2 %copy-done = bf16[2,4,1,2,128,256]{5,4,3,2,1,0:T(8,128)(2,1)S(1)} copy-done((bf16[2,4,1,2,128,256]{5,4,3,2,1,0:T(8,128)(2,1)S(1)}, bf16[2,4,1,2,128,256]{5,4,3,2,1,0:T(8,128)(2,1)}, u32[]{:S(2)}) %copy-start) | copy-done | bytes 1048600
  1.9 0.0 copy-start.1
  1.9 1.2 %copy-done.1 = bf16[2,4,1,2,128,256]{5,4,3,2,1,0:T(8,128)(2,1)S(1)} copy-done((bf16[2,4,1,2,128,256]{5,4,3,2,1,0:T(8,128)(2,1)S(1)}, bf16[2,4,1,2,128,256]{5,4,3,2,1,0:T(8,128)(2,1)}, u32[]{:S(2)}) %copy-start.1) | copy-done | bytes 1048600
  3.1 0.0 copy-start.2
  3.1 1.1 %copy-done.2 = bf16[2,3,2,128,256]{4,3,2,1,0:T(8,128)(2,1)S(1)} copy-done((bf16[2,3,2,128,256]{4,3,2,1,0:T(8,128)(2,1)S(1)}, bf16[2,3,2,128,256]{4,3,2,1,0:T(8,128)(2,1)}, u32[]{:S(2)}) %copy-start.2) | copy-done | bytes 786456
  4.2 0.0 copy-start.3
  4.2 1.0 %copy-done.3 = s32[2,4,1,2,2,16,256]{6,5,4,3,2,1,0:T(8,128)S(1)} copy-done((s32[2,4,1,2,2,16,256]{6,5,4,3,2,1,0:T(8,128)S(1)}, s32[2,4,1,2,2,16,256]{6,5,4,3,2,1,0:T(8,128)}, u32[]{:S(2)}) %copy-start.3) | copy-done | bytes 524312
  5.3 0.0 copy-start.4
  5.3 0.9 copy-done.4
  6.2 93.8 %shard_map.77 = (bf16[2,4,1,2,128,256]{5,4,3,2,1,0:T(8,128)(2,1)S(1)}, f32[1,2,288,256]{3,2,1,0:T(8,128)S(1)}) custom-call(bf16[2,1,2,128,256]{4,3,2,1,0:T(8,128)(2,1)S(1)} %copy-done.4, bf16[2,3,2,128,256]{4,3,2,1,0:T(8,128)(2,1)S(1)} %copy-done.2, bf16[2,4,1,2,128,256]{5,4,3,2,1,0:T(8,128)(2,1)S(1)} %copy-done, ...), custom_call_target="tpu_custom_call" | custom-call | tf_op jit(solution)/shard_map/pallas_call | solution.py:361
  100.0 1.0 copy.10
  100.9 0.8 copy.11
Async XLA Ops:
  0.6 1.2 %copy-start = (bf16[2,4,1,2,128,256]{5,4,3,2,1,0:T(8,128)(2,1)S(1)}, bf16[2,4,1,2,128,256]{5,4,3,2,1,0:T(8,128)(2,1)}, u32[]{:S(2)}) copy-start(bf16[2,4,1,2,128,256]{5,4,3,2,1,0:T(8,128)(2,1)} %inputs_ref.1) | copy-start | bytes 3145732
  1.9 1.2 %copy-start.1 = (bf16[2,4,1,2,128,256]{5,4,3,2,1,0:T(8,128)(2,1)S(1)}, bf16[2,4,1,2,128,256]{5,4,3,2,1,0:T(8,128)(2,1)}, u32[]{:S(2)}) copy-start(bf16[2,4,1,2,128,256]{5,4,3,2,1,0:T(8,128)(2,1)} %hidden_ref.1) | copy-start | bytes 3145732
  3.1 1.1 %copy-start.2 = (bf16[2,3,2,128,256]{4,3,2,1,0:T(8,128)(2,1)S(1)}, bf16[2,3,2,128,256]{4,3,2,1,0:T(8,128)(2,1)}, u32[]{:S(2)}) copy-start(bf16[2,3,2,128,256]{4,3,2,1,0:T(8,128)(2,1)} %fresh_ref.1) | copy-start | bytes 2359300
  4.2 1.0 %copy-start.3 = (s32[2,4,1,2,2,16,256]{6,5,4,3,2,1,0:T(8,128)S(1)}, s32[2,4,1,2,2,16,256]{6,5,4,3,2,1,0:T(8,128)}, u32[]{:S(2)}) copy-start(s32[2,4,1,2,2,16,256]{6,5,4,3,2,1,0:T(8,128)} %masks_ref.1) | copy-start | bytes 1572868
  5.3 0.9 copy-start.4

commit v3 on v2

--- a/solution.py
+++ b/solution.py
@@ -368,7 +368,7 @@
         out_specs=(VMEM, VMEM),
         scratch_shapes=scratch,
         compiler_params=pltpu.CompilerParams(
-            collective_id=0, has_side_effects=True, vmem_limit_bytes=48 << 20
+            collective_id=0, has_side_effects=True, vmem_limit_bytes=67043328
         ),
     )(in_flight, fresh, saved_inputs, saved_hidden, masks, weights)
 

time: 102 us -> 98.9 us (0.970)
  local copies, waits for them, and re-layouts: 7.35 us -> 3.17 us
  Pallas kernels: 93.8 us -> 94.9 us
    unnamed x12 -> x4, local copies, waits for them, and re-layouts: 7.35 us -> 3.17 us
    pallas_call x1, Pallas kernels: 93.8 us -> 94.9 us  [per_device(): pl.pallas_call(relay_kernel, out_shape=(jax.ShapeDtypeStruct(saved_inputs...]
where the time goes in v3:
time: 98.9 us; the launch traced here: 98.7 us
  Pallas kernels  94.9 us (96%)
  local copies, waits for them, and re-layouts  3.17 us (3%)
    pallas_call x1, Pallas kernels, per_device(): pl.pallas_call(relay_kernel, out_shape=(jax.ShapeDtypeStruct(saved_inputs...  94.9 us
    unnamed x4, local copies, waits for them, and re-layouts  3.17 us

profile of v3, /device:TPU:24, one launch (start us, length us, event | category | flops | bytes accessed | tf_op | source)
XLA Modules:
  0.0 98.7 jit_solution(2711923958886362860)
XLA Ops:
  0.6 94.9 %shard_map.77 = (bf16[2,4,1,2,128,256]{5,4,3,2,1,0:T(8,128)(2,1)}, f32[1,2,288,256]{3,2,1,0:T(8,128)}) custom-call(bf16[2,1,2,128,256]{4,3,2,1,0:T(8,128)(2,1)} %flight_ref.1, bf16[2,3,2,128,256]{4,3,2,1,0:T(8,128)(2,1)} %fresh_ref.1, bf16[2,4,1,2,128,256]{5,4,3,2,1,0:T(8,128)(2,1)} %inputs_ref.1, bf16[2,4,1,2,128,256]{5,4,3,2,1,0:T(8,128)(2,1)} %hidden_ref.1, ...), custom_call_target="tpu_custom_call" | custom-call | tf_op jit(solution)/shard_map/pallas_call | solution.py:361
  95.5 0.0 copy-start
  95.5 2.3 %copy.10 = bf16[2,4,1,2,128,256]{5,4,3,2,1,0:T(8,128)(2,1)} copy(bf16[2,4,1,2,128,256]{5,4,3,2,1,0:T(8,128)(2,1)} %get-tuple-element.4) | data formatting | bytes 2097152
  97.9 0.0 copy-done
  97.9 0.8 copy.11
Async XLA Ops:
  95.5 2.4 %copy-start = (f32[1,2,288,256]{3,2,1,0:T(8,128)S(1)}, f32[1,2,288,256]{3,2,1,0:T(8,128)}, u32[]{:S(2)}) copy-start(f32[1,2,288,256]{3,2,1,0:T(8,128)} %get-tuple-element.5) | copy-start | bytes 1769476

commit v4 on v3

--- a/solution.py
+++ b/solution.py
@@ -234,6 +234,9 @@
             value = value + chip_in[k, d].astype(F32)
         wgrads_ref[0, k] = value * scale
 
+    def back_copy(t):
+        return copy(produced.at[t, 1], grads_ref.at[1, t, 0], back_sem.at[t], other)
+
     is_last = sec == sections - 1
     hands = [None, None]
     backs = []
@@ -263,6 +266,8 @@
                     gate(t, r, lambda i: handed[t - 1, r, i])
 
             pairs.append(exchange(1, t, r))
+            if r == 1 and t > 0:
+                backs.append(send(back_copy(t - 1)))
             if r == 0:
                 for c in queue[t] if t < len(queue) else []:
                     send(c)
@@ -301,7 +306,8 @@
                     (jnp.maximum(sec - 1, 0), row),
                 )
                 send(hands[r], sec > 0)
-        backs.append(send(copy(produced.at[t, 1], grads_ref.at[1, t, 0], back_sem.at[t], other)))
+        if t == ticks - 1:
+            backs.append(send(back_copy(t)))
         if t < ticks - 1:
             hidden_copies[t].wait_recv()
             if t == 0:

time: 98.9 us -> 98.7 us (level)
  Pallas kernels: 94.9 us -> 93.9 us
where the time goes in v4:
time: 98.7 us; the launch traced here: 97.8 us
  Pallas kernels  93.9 us (95%)
  local copies, waits for them, and re-layouts  3.17 us (3%)
    pallas_call x1, Pallas kernels, per_device(): pl.pallas_call(relay_kernel, out_shape=(jax.ShapeDtypeStruct(saved_inputs...  93.9 us
    unnamed x4, local copies, waits for them, and re-layouts  3.17 us

profile of v4, /device:TPU:24, one launch (start us, length us, event | category | flops | bytes accessed | tf_op | source)
XLA Modules:
  0.0 97.8 jit_solution(4908205357086802132)
XLA Ops:
  0.6 93.9 %shard_map.77 = (bf16[2,4,1,2,128,256]{5,4,3,2,1,0:T(8,128)(2,1)}, f32[1,2,288,256]{3,2,1,0:T(8,128)}) custom-call(bf16[2,1,2,128,256]{4,3,2,1,0:T(8,128)(2,1)} %flight_ref.1, bf16[2,3,2,128,256]{4,3,2,1,0:T(8,128)(2,1)} %fresh_ref.1, bf16[2,4,1,2,128,256]{5,4,3,2,1,0:T(8,128)(2,1)} %inputs_ref.1, bf16[2,4,1,2,128,256]{5,4,3,2,1,0:T(8,128)(2,1)} %hidden_ref.1, ...), custom_call_target="tpu_custom_call" | custom-call | tf_op jit(solution)/shard_map/pallas_call | solution.py:367
  94.6 0.0 copy-start
  94.6 2.3 %copy.10 = bf16[2,4,1,2,128,256]{5,4,3,2,1,0:T(8,128)(2,1)} copy(bf16[2,4,1,2,128,256]{5,4,3,2,1,0:T(8,128)(2,1)} %get-tuple-element.4) | data formatting | bytes 2097152
  96.9 0.0 copy-done
  96.9 0.8 copy.11
Async XLA Ops:
  94.6 2.4 %copy-start = (f32[1,2,288,256]{3,2,1,0:T(8,128)S(1)}, f32[1,2,288,256]{3,2,1,0:T(8,128)}, u32[]{:S(2)}) copy-start(f32[1,2,288,256]{3,2,1,0:T(8,128)} %get-tuple-element.5) | copy-start | bytes 1769476
